TPU v7x, 32 devices: a whole 2x2x4 slice. The times are simulated.
32 devices in a mesh: slab: 2 (over x), wide: 16 (over z, y, core).
Axes of the slice: x: 2, y: 2, z: 4, core: 2. Of those that a mesh axis runs over, the one named last changes fastest.
Arguments:
- slc: bfloat16 [128, 512, 2, 512], P('wide', 'slab'), parts along dimension 1, may hold values from -10 to 10
- offsets: bfloat16 [128, 512], P('wide', 'slab'), parts along dimension 1, may hold values from -0.5 to 0.5
- row_start: int32 [128], replicated, may hold values from 0 to 127
- row_stop: int32 [128], replicated, may hold values from 385 to 512
- pairs: int32 [64, 2], replicated, may hold values from 0 to 127, as said below
Outputs:
- coherence: bfloat16 [1024, 2, 128, 128], P(('slab', 'wide')), parts along dimension 0
- flattened: float32 [1024, 2, 64], P(('slab', 'wide')), parts along dimension 0
- ramps: float32 [128, 2, 3], P(('slab', 'wide')), parts along dimension 0
There are 2 independent parts, one for each index of `slab`. A program takes and returns all parts, laid end to end along the dimension named above; an argument that names none is the same for every part. Nothing has to cross between parts.
Inputs may be any that keep to these rules, and one draw needn't show every extreme that they name: `pairs`: each row names two different dates.
All inputs are finite; a program needn't handle non-finite values.
Results may differ from a plain program's by a relative error of at most 0.0098.
Values may be sent and summed in bfloat16 or wider, within the bound.
A program may use at most 128 MiB of HBM per device.

v0:
```python
import functools
import math

import jax
import jax.numpy as jnp
import numpy as np
from jax import lax
from jax.experimental import pallas as pl
from jax.experimental.pallas import tpu as pltpu
from jax.sharding import PartitionSpec as P

AZ = 512
LOOK_AZ = 16
LOOK_RG = 16
RADIX = 4
PART = AZ // RADIX
LINE_CELLS = AZ // LOOK_AZ
PHASES = 4
HIGH = 8
LOW = PART // HIGH

damping = 1.0


def host_tables():
    forward, inverse = [], []
    m = np.arange(PART)
    for r in range(RADIX):
        product = ((RADIX * m + r)[:, None] * m[None, :]) % AZ
        angles = product * (2.0 * math.pi / AZ)
        cosine, sine = np.cos(angles), np.sin(angles)
        forward.append(np.block([[cosine, sine], [-sine, cosine]]))
        inverse.append(np.block([[cosine.T, -sine.T], [sine.T, cosine.T]]))
    forward = jnp.asarray(np.stack(forward), jnp.float32).astype(jnp.bfloat16)
    inverse = jnp.asarray(np.stack(inverse), jnp.float32).astype(jnp.bfloat16)
    inverse = inverse * jnp.asarray(1.0 / AZ, jnp.bfloat16)
    return forward, inverse


def split_table(dates):
    table = np.zeros((2, dates, dates, 2), np.float32)
    for q in range(2):
        table[q, np.arange(dates), np.arange(dates), q] = 1.0
    return jnp.asarray(table.reshape(2 * dates, 2 * dates)).astype(jnp.bfloat16)


def frequency_factors():
    high = np.arange(HIGH)
    high = np.where(high < HIGH // 2, high, high - HIGH) * (RADIX * LOW)
    low = np.arange(LOW) * RADIX
    rest = np.concatenate([np.arange(RADIX), np.zeros(4)])
    factors = np.concatenate([high, low, rest]).astype(np.float32)
    return jnp.asarray(factors[:, None])


def resample_kernel(
    n, slc_ref, placed_ref, split_ref, forward_ref, inverse_ref, factor_ref, start_ref, stop_ref,
    out_ref, held, shifts, theta, mask, send_sem, recv_sem, osend_sem, orecv_sem, own_sem,
):
    me = lax.axis_index("wide")
    dates_here = slc_ref.shape[0]
    dates = held.shape[0]
    columns = held.shape[1]
    step = columns // PHASES
    barrier = pltpu.get_barrier_semaphore()

    def other(k):
        return lax.rem(me + k, n)

    def greet(k, carry):
        pl.semaphore_signal(barrier, inc=1, device_id={"wide": other(k)}, device_id_type=pl.DeviceIdType.MESH)
        return carry

    lax.fori_loop(1, n, greet, 0)
    mine = pl.ds(me * dates_here, dates_here)
    own = pltpu.make_async_copy(
        slc_ref.at[:, pl.ds(me * columns, columns)], held.at[mine], own_sem.at[0]
    )
    own.start()
    own_shift = pltpu.make_async_copy(placed_ref.at[me], shifts.at[me], own_sem.at[1])
    own_shift.start()

    row = lax.broadcasted_iota(jnp.int32, (dates, AZ), 1)
    valid = (row >= start_ref[...]) & (row < stop_ref[...])
    mask[...] = jnp.where(valid, 1.0, 0.0)
    pl.semaphore_wait(barrier, n - 1)

    def shift_copy(k):
        return pltpu.make_async_remote_copy(
            src_ref=placed_ref.at[other(k)], dst_ref=shifts.at[me],
            send_sem=osend_sem.at[k], recv_sem=orecv_sem.at[k],
            device_id={"wide": other(k)}, device_id_type=pl.DeviceIdType.MESH,
        )

    def sample_copy(phase, k):
        return pltpu.make_async_remote_copy(
            src_ref=slc_ref.at[:, pl.ds(other(k) * columns + phase * step, step)],
            dst_ref=held.at[mine, pl.ds(phase * step, step)],
            send_sem=send_sem.at[phase, k], recv_sem=recv_sem.at[phase, k],
            device_id={"wide": other(k)}, device_id_type=pl.DeviceIdType.MESH,
        )

    def start_shift(k, carry):
        shift_copy(k).start()
        return carry

    lax.fori_loop(1, n, start_shift, 0)

    def start_sample(i, carry):
        sample_copy(i // (n - 1), i % (n - 1) + 1).start()
        return carry

    lax.fori_loop(0, PHASES * (n - 1), start_sample, 0)
    own.wait()
    own_shift.wait()

    def wait_shift(k, carry):
        shift_copy(k).wait()
        return carry

    lax.fori_loop(1, n, wait_shift, 0)
    total = jnp.sum(shifts[...].astype(jnp.float32), 0)
    theta[...] = total * (-2.0 * math.pi / AZ)

    def column_pair(pair, carry):
        parts = [[] for _ in range(RADIX)]
        for side in range(2):
            column = pair * 2 + side
            packed = jnp.concatenate(
                [held[:, column, j].reshape(2 * dates, PART) for j in range(RADIX)], 1
            )
            samples = jnp.dot(split_ref[...], packed, preferred_element_type=jnp.float32)
            real = samples[:dates] * mask[...]
            imag = samples[dates:] * mask[...]
            a = [real[:, j * PART : (j + 1) * PART] for j in range(RADIX)]
            b = [imag[:, j * PART : (j + 1) * PART] for j in range(RADIX)]
            ap, am, bp, bm = a[0] + a[2], a[0] - a[2], b[0] + b[2], b[0] - b[2]
            cp, cm, dp, dm = a[1] + a[3], a[1] - a[3], b[1] + b[3], b[1] - b[3]
            groups = ((ap + cp, bp + dp), (am + dm, bm - cm), (ap - cp, bp - dp), (am - dm, bm + cm))
            for r in range(RADIX):
                parts[r].append(jnp.concatenate(groups[r], 1).astype(jnp.bfloat16))
        angle = jnp.concatenate(
            [theta[pl.ds(pair * 2, 1), :], theta[pl.ds(pair * 2 + 1, 1), :]], 1
        )
        wide = angle.shape[1]
        rotation = factor_ref[...] * angle
        cosine, sine = jnp.cos(rotation), jnp.sin(rotation)
        hc, hs = cosine[:HIGH][:, None, :], sine[:HIGH][:, None, :]
        lc, ls = cosine[HIGH : HIGH + LOW][None], sine[HIGH : HIGH + LOW][None]
        base_cos = (hc * lc - hs * ls).reshape(PART, wide)
        base_sin = (hc * ls + hs * lc).reshape(PART, wide)
        restored = []
        for r in range(RADIX):
            spectrum = lax.dot_general(
                forward_ref[r], jnp.concatenate(parts[r], 0), (((1,), (1,)), ((), ())),
                preferred_element_type=jnp.float32,
            )
            at = HIGH + LOW + r
            rc, rs = cosine[at : at + 1], sine[at : at + 1]
            if r == 0:
                turn_cos, turn_sin = base_cos, base_sin
            else:
                turn_cos = base_cos * rc - base_sin * rs
                turn_sin = base_cos * rs + base_sin * rc
            sr, si = spectrum[:PART], spectrum[PART:]
            turned = jnp.concatenate(
                [sr * turn_cos - si * turn_sin, sr * turn_sin + si * turn_cos], 0
            ).astype(jnp.bfloat16)
            restored.append(jnp.dot(inverse_ref[r], turned, preferred_element_type=jnp.float32))
        x = [v[:PART] for v in restored]
        y = [v[PART:] for v in restored]
        ap, am, bp, bm = x[0] + x[2], x[0] - x[2], y[0] + y[2], y[0] - y[2]
        cp, cm, dp, dm = x[1] + x[3], x[1] - x[3], y[1] + y[3], y[1] - y[3]
        lines = ((ap + cp, bp + dp), (am - dm, bm + cm), (ap - cp, bp - dp), (am + dm, bm - cm))
        cells = PART // LOOK_AZ
        for j in range(RADIX):
            for q in range(2):
                value = lines[j][q].astype(jnp.bfloat16)
                for side in range(2):
                    place = pl.multiple_of((pair * 2 + side) * LOOK_AZ, LOOK_AZ)
                    out_ref[
                        j * cells : (j + 1) * cells, pl.ds(place, LOOK_AZ), q * dates : (q + 1) * dates
                    ] = value[:, side * dates : (side + 1) * dates].reshape(cells, LOOK_AZ, dates)
        return carry

    def one_phase(phase, carry):
        def wait_sample(k, inner):
            sample_copy(phase, k).wait()
            return inner

        lax.fori_loop(1, n, wait_sample, 0)
        lax.fori_loop(phase * (step // 2), (phase + 1) * (step // 2), column_pair, 0)
        return carry

    lax.fori_loop(0, PHASES, one_phase, 0)


def cells_kernel(first_ref, second_ref, pixels_ref, coherence_ref, chosen_ref):
    dates = pixels_ref.shape[2] // 2
    eye = lax.broadcasted_iota(jnp.int32, (dates, dates), 0) == lax.broadcasted_iota(
        jnp.int32, (dates, dates), 1
    )
    for g in range(pixels_ref.shape[0]):
        pixels = pixels_ref[g]
        gram = lax.dot_general(
            pixels, pixels, (((0,), (0,)), ((), ())), preferred_element_type=jnp.float32
        )
        real = gram[:dates, :dates] + gram[dates:, dates:]
        imag = gram[dates:, :dates] - gram[:dates, dates:]
        diagonal = jnp.where(eye, real, 0.0)
        row = lax.rsqrt(jnp.sum(diagonal, 0, keepdims=True) + damping)
        column = lax.rsqrt(jnp.sum(diagonal, 1, keepdims=True) + damping)
        scale = row * column
        for q, value in enumerate((real, imag)):
            gamma = (value * scale).astype(jnp.bfloat16)
            coherence_ref[g, q] = gamma
            picked = jnp.dot(gamma, second_ref[...], preferred_element_type=jnp.float32)
            chosen_ref[q, g : g + 1, :] = jnp.sum(picked * first_ref[...], 0, keepdims=True)


def ramps_kernel(n, chosen_ref, flat_ref, ramps_ref, sums, sum_send, sum_recv):
    me = lax.axis_index("wide")
    cells, pairs = chosen_ref.shape[1], chosen_ref.shape[2]
    barrier = pltpu.get_barrier_semaphore()

    def other(k):
        return lax.rem(me + k, n)

    def greet(k, carry):
        pl.semaphore_signal(barrier, inc=1, device_id={"wide": other(k)}, device_id_type=pl.DeviceIdType.MESH)
        return carry

    lax.fori_loop(1, n, greet, 0)
    across = (
        lax.broadcasted_iota(jnp.int32, (cells, pairs), 0).astype(jnp.float32) + 0.5
    ) / cells - 0.5
    real, imag = chosen_ref[0], chosen_ref[1]
    weights = 0.1 + real * real + imag * imag
    tilted = weights * across

    def down(value):
        return jnp.sum(value, 0, keepdims=True)

    sums[me] = jnp.concatenate(
        [
            down(weights), down(tilted), down(tilted * across),
            down(weights * real), down(tilted * real),
            down(weights * imag), down(tilted * imag),
            jnp.zeros((1, pairs), jnp.float32),
        ],
        0,
    )
    pl.semaphore_wait(barrier, n - 1)

    def sum_copy(k):
        return pltpu.make_async_remote_copy(
            src_ref=sums.at[me], dst_ref=sums.at[me],
            send_sem=sum_send.at[k], recv_sem=sum_recv.at[k],
            device_id={"wide": other(k)}, device_id_type=pl.DeviceIdType.MESH,
        )

    def start(k, carry):
        sum_copy(k).start()
        return carry

    def finish(k, carry):
        sum_copy(k).wait()
        return carry

    lax.fori_loop(1, n, start, 0)
    lax.fori_loop(1, n, finish, 0)
    plain = jnp.zeros((8, pairs), jnp.float32)
    once = plain
    twice = plain
    for source in range(n):
        along = (source + 0.5) / n - 0.5
        value = sums[source]
        plain = plain + value
        once = once + value * along
        twice = twice + value * (along * along)

    n00, n01, n11 = plain[0:1], plain[1:2], plain[2:3]
    n02, n12, n22 = once[0:1], once[1:2], twice[0:1]
    adj00 = n11 * n22 - n12 * n12
    adj01 = n02 * n12 - n01 * n22
    adj02 = n01 * n12 - n02 * n11
    adj11 = n00 * n22 - n02 * n02
    adj12 = n01 * n02 - n00 * n12
    adj22 = n00 * n11 - n01 * n01
    determinant = n00 * adj00 + n01 * adj01 + n02 * adj02
    my_along = (me.astype(jnp.float32) + 0.5) / n - 0.5
    rows = []
    for q, value in enumerate((real, imag)):
        at = 3 + 2 * q
        t0, t1, t2 = plain[at : at + 1], plain[at + 1 : at + 2], once[at : at + 1]
        b0 = (adj00 * t0 + adj01 * t1 + adj02 * t2) / determinant
        b1 = (adj01 * t0 + adj11 * t1 + adj12 * t2) / determinant
        b2 = (adj02 * t0 + adj12 * t1 + adj22 * t2) / determinant
        rows += [b0, b1, b2]
        flat_ref[:, q, :] = value - (b0 + across * b1 + my_along * b2)
    ramps_ref[...] = jnp.concatenate(rows + [jnp.zeros((2, pairs), jnp.float32)], 0)


def local(slc, offsets, row_start, row_stop, pairs):
    n = lax.axis_size("wide")
    me = lax.axis_index("wide")
    dates_here, all_columns = slc.shape[0], slc.shape[1]
    dates = row_start.shape[0]
    columns = all_columns // n
    pair_count = pairs.shape[0]
    samples = slc.reshape(dates_here, all_columns, 2, RADIX, PART).transpose(0, 1, 3, 2, 4)
    spot = jnp.arange(dates_here, dtype=jnp.int32)[:, None] + me * dates_here
    onehot = (spot == jnp.arange(dates, dtype=jnp.int32)[None, :]).astype(jnp.bfloat16)
    placed = jnp.einsum("dc,dl->cl", offsets, onehot, preferred_element_type=jnp.float32)
    placed = placed.astype(jnp.bfloat16).reshape(n, columns, dates)
    forward, inverse = host_tables()
    vmem = pl.BlockSpec(memory_space=pltpu.VMEM)
    anywhere = pl.BlockSpec(memory_space=pl.ANY)
    pixels = pl.pallas_call(
        functools.partial(resample_kernel, n),
        out_shape=jax.ShapeDtypeStruct((LINE_CELLS, columns * LOOK_AZ, 2 * dates), jnp.bfloat16),
        in_specs=[anywhere, anywhere] + [vmem] * 6,
        out_specs=vmem,
        scratch_shapes=[
            pltpu.VMEM((dates, columns, RADIX, 2, PART), jnp.bfloat16),
            pltpu.VMEM((n, columns, dates), jnp.bfloat16),
            pltpu.VMEM((columns, dates), jnp.float32),
            pltpu.VMEM((dates, AZ), jnp.float32),
            pltpu.SemaphoreType.DMA((PHASES, n)),
            pltpu.SemaphoreType.DMA((PHASES, n)),
            pltpu.SemaphoreType.DMA((n,)),
            pltpu.SemaphoreType.DMA((n,)),
            pltpu.SemaphoreType.DMA((2,)),
        ],
        compiler_params=pltpu.CompilerParams(
            collective_id=0, has_side_effects=True, vmem_limit_bytes=48 << 20
        ),
    )(
        samples, placed, split_table(dates), forward, inverse, frequency_factors(),
        row_start[:, None], row_stop[:, None],
    )

    date = jnp.arange(dates, dtype=jnp.int32)[:, None]
    first = (date == pairs[:, 0][None, :]).astype(jnp.float32)
    second = (date == pairs[:, 1][None, :]).astype(jnp.bfloat16)
    batch = 8
    coherent, chosen = pl.pallas_call(
        cells_kernel,
        grid=(LINE_CELLS // batch,),
        in_specs=[
            pl.BlockSpec((dates, pair_count), lambda i: (0, 0)),
            pl.BlockSpec((dates, pair_count), lambda i: (0, 0)),
            pl.BlockSpec((batch, columns * LOOK_AZ, 2 * dates), lambda i: (i, 0, 0)),
        ],
        out_specs=[
            pl.BlockSpec((batch, 2, dates, dates), lambda i: (i, 0, 0, 0)),
            pl.BlockSpec((2, batch, pair_count), lambda i: (0, i, 0)),
        ],
        out_shape=[
            jax.ShapeDtypeStruct((LINE_CELLS, 2, dates, dates), jnp.bfloat16),
            jax.ShapeDtypeStruct((2, LINE_CELLS, pair_count), jnp.float32),
        ],
    )(first, second, pixels)

    flattened, ramps = pl.pallas_call(
        functools.partial(ramps_kernel, n),
        in_specs=[vmem],
        out_specs=[vmem, vmem],
        out_shape=[
            jax.ShapeDtypeStruct((LINE_CELLS, 2, pair_count), jnp.float32),
            jax.ShapeDtypeStruct((8, pair_count), jnp.float32),
        ],
        scratch_shapes=[
            pltpu.VMEM((n, 8, pair_count), jnp.float32),
            pltpu.SemaphoreType.DMA((n,)),
            pltpu.SemaphoreType.DMA((n,)),
        ],
        compiler_params=pltpu.CompilerParams(collective_id=1, has_side_effects=True),
    )(chosen)
    pairs_here = pair_count // n
    own = lax.dynamic_slice_in_dim(ramps, me * pairs_here, pairs_here, 1)[:6]
    return coherent, flattened, own.T.reshape(pairs_here, 2, 3)


def solution(mesh):
    placed = (P("wide", "slab", None, None), P("wide", "slab"), P(), P(), P())
    return jax.shard_map(
        local,
        mesh=mesh,
        in_specs=placed,
        out_specs=(
            P(("slab", "wide"), None, None, None),
            P(("slab", "wide"), None, None),
            P(("slab", "wide"), None, None),
        ),
        check_vma=False,
    )
```

profile of v0, /device:TPU:0, one launch (start us, length us, event | category | flops | bytes accessed | tf_op | source)
XLA Modules:
  0.0 131.7 jit_solution(10049946813055519553)
XLA Ops:
  0.6 0.0 copy-start
  0.7 0.8 slice_bitcast_fusion.1
  1.4 0.0 copy-done
  1.4 0.3 fusion
  1.7 0.1 copy.17
  1.8 0.8 copy.18.start_ref
  2.6 0.8 copy.19.stop_ref
  3.4 0.7 fusion.1
  4.0 0.0 copy-start.2
  4.0 1.0 copy-done.2
  5.1 0.0 copy-start.3
  5.1 1.0 copy-done.3
  6.1 0.0 copy-start.4
  6.1 0.9 copy-done.4
  7.0 0.0 copy-start.5
  7.0 0.7 copy-done.5
  7.7 93.2 %shard_map.112.pixels_ref = bf16[32,256,256]{2,1,0:T(8,128)(2,1)S(1)} custom-call(bf16[8,256,4,2,128]{4,3,2,1,0:T(2,128)(2,1)} %bitcast.18, bf16[16,16,128]{2,1,0:T(8,128)(2,1)S(1)} %bitcast.17, bf16[256,256]{1,0:T(8,128)(2,1)S(1)} %copy-done.4, bf16[4,256,256]{2,1,0:T(8,128)(2,1)S(1)} %copy-done.3, bf16[4,256,256]{2,1,0:T(8,128)(2,1)S(1)} %copy-done.2, ...), custom_call_target="tpu_custom_call" | custom-call | tf_op jit(solution)/shard_map/pallas_call | solution.py:319
  100.9 0.0 copy-start.1
  100.9 1.9 %copy-done.1 = bf16[32,256,256]{2,1,0:T(8,128)(2,1)} copy-done((bf16[32,256,256]{2,1,0:T(8,128)(2,1)}, bf16[32,256,256]{2,1,0:T(8,128)(2,1)S(1)}, u32[]{:S(2)}) %copy-start.1) | copy-done | bytes 4194328
  102.9 9.5 %shard_map.113 = (bf16[32,2,128,128]{3,2,1,0:T(8,128)(2,1)}, f32[2,32,64]{2,1,0:T(8,128)}) custom-call(f32[128,64]{1,0:T(8,128)} %get-tuple-element.19.first_ref, bf16[128,64]{1,0:T(8,128)(2,1)} %get-tuple-element.20.second_ref, bf16[32,256,256]{2,1,0:T(8,128)(2,1)} %copy-done.1), custom_call_target="tpu_custom_call" | custom-call | tf_op jit(solution)/shard_map/pallas_call | solution.py:347
  112.4 16.6 %shard_map.114 = (f32[32,2,64]{2,1,0:T(2,128)}, f32[8,64]{1,0:T(8,128)}) custom-call(f32[2,32,64]{2,1,0:T(8,128)} %get-tuple-element.8.chosen_ref), custom_call_target="tpu_custom_call" | custom-call | tf_op jit(solution)/shard_map/pallas_call | solution.py:365
  129.0 0.8 constant_dynamic-slice_fusion
  129.8 0.6 copy.21
  130.4 1.4 %copy.25 = f32[32,2,64]{2,1,0:T(2,128)} copy(f32[32,2,64]{2,1,0:T(2,128)} %get-tuple-element.25) | data formatting | bytes 32768
  (3 shorter events, 0.0 us)
Async XLA Ops:
  0.6 0.8 copy-start
  4.0 1.0 copy-start.2
  5.1 1.0 copy-start.3
  6.1 0.9 copy-start.4
  7.0 0.7 copy-start.5
  100.9 1.9 %copy-start.1 = (bf16[32,256,256]{2,1,0:T(8,128)(2,1)}, bf16[32,256,256]{2,1,0:T(8,128)(2,1)S(1)}, u32[]{:S(2)}) copy-start(bf16[32,256,256]{2,1,0:T(8,128)(2,1)S(1)} %shard_map.112.pixels_ref) | copy-start | bytes 12582916
where the time goes:
time: 132 us
  Pallas kernels  119 us (90%)
  local copies, waits for them, and re-layouts  10.8 us (8%)
    pallas_call x1, Pallas kernels, local(): pl.pallas_call(functools.partial(resample_kernel, n), out_shape=jax.Shape...  93.2 us
    pallas_call x1, Pallas kernels, local(): pl.pallas_call(functools.partial(ramps_kernel, n), in_specs=[vmem], out_s...  16.6 us
    pallas_call x1, Pallas kernels, local(): pl.pallas_call(cells_kernel, grid=(LINE_CELLS // batch,), in_specs=[pl.Bl...  9.54 us
    unnamed x14, local copies, waits for them, and re-layouts  7.61 us

commit v1 on v0

--- a/solution.py
+++ b/solution.py
@@ -15,7 +15,7 @@
 RADIX = 4
 PART = AZ // RADIX
 LINE_CELLS = AZ // LOOK_AZ
-PHASES = 4
+PHASES = 8
 HIGH = 8
 LOW = PART // HIGH
 
@@ -53,9 +53,11 @@
     return jnp.asarray(factors[:, None])
 
 
-def resample_kernel(
-    n, slc_ref, placed_ref, split_ref, forward_ref, inverse_ref, factor_ref, start_ref, stop_ref,
-    out_ref, held, shifts, theta, mask, send_sem, recv_sem, osend_sem, orecv_sem, own_sem,
+def stack_kernel(
+    n, slc_ref, placed_ref, split_hbm, forward_hbm, inverse_hbm, factor_ref, bounds_ref, pairs_ref,
+    coherence_ref, flat_ref, ramps_ref,
+    held, shifts, theta, mask, pixels_ref, coherent, chosen, sums, split_ref, forward_ref, inverse_ref,
+    send_sem, recv_sem, osend_sem, orecv_sem, own_sem, out_sem, sum_send, sum_recv,
 ):
     me = lax.axis_index("wide")
     dates_here = slc_ref.shape[0]
@@ -64,14 +66,25 @@
     step = columns // PHASES
     barrier = pltpu.get_barrier_semaphore()
 
+    half = n // 2
+
     def other(k):
-        return lax.rem(me + k, n)
+        inside = (k + 1) % 2
+        return ((me // half + 1 - inside) % 2) * half + (me + (k - 1) // 2 + inside) % half
 
     def greet(k, carry):
         pl.semaphore_signal(barrier, inc=1, device_id={"wide": other(k)}, device_id_type=pl.DeviceIdType.MESH)
         return carry
 
     lax.fori_loop(1, n, greet, 0)
+    tables = [
+        pltpu.make_async_copy(source, target, own_sem.at[2 + i])
+        for i, (source, target) in enumerate(
+            ((split_hbm, split_ref), (forward_hbm, forward_ref), (inverse_hbm, inverse_ref))
+        )
+    ]
+    for table in tables:
+        table.start()
     mine = pl.ds(me * dates_here, dates_here)
     own = pltpu.make_async_copy(
         slc_ref.at[:, pl.ds(me * columns, columns)], held.at[mine], own_sem.at[0]
@@ -80,9 +93,6 @@
     own_shift = pltpu.make_async_copy(placed_ref.at[me], shifts.at[me], own_sem.at[1])
     own_shift.start()
 
-    row = lax.broadcasted_iota(jnp.int32, (dates, AZ), 1)
-    valid = (row >= start_ref[...]) & (row < stop_ref[...])
-    mask[...] = jnp.where(valid, 1.0, 0.0)
     pl.semaphore_wait(barrier, n - 1)
 
     def shift_copy(k):
@@ -111,8 +121,19 @@
         return carry
 
     lax.fori_loop(0, PHASES * (n - 1), start_sample, 0)
+    eye = lax.broadcasted_iota(jnp.int32, (dates, dates), 0) == lax.broadcasted_iota(
+        jnp.int32, (dates, dates), 1
+    )
+    bounds = [
+        jnp.sum(jnp.where(eye, bounds_ref[i : i + 1, :].astype(jnp.float32), 0.0), 1, keepdims=True)
+        for i in range(2)
+    ]
+    row = lax.broadcasted_iota(jnp.int32, (dates, AZ), 1).astype(jnp.float32)
+    mask[...] = jnp.where((row >= bounds[0]) & (row < bounds[1]), 1.0, 0.0)
     own.wait()
     own_shift.wait()
+    for table in tables:
+        table.wait()
 
     def wait_shift(k, carry):
         shift_copy(k).wait()
@@ -178,7 +199,7 @@
                 value = lines[j][q].astype(jnp.bfloat16)
                 for side in range(2):
                     place = pl.multiple_of((pair * 2 + side) * LOOK_AZ, LOOK_AZ)
-                    out_ref[
+                    pixels_ref[
                         j * cells : (j + 1) * cells, pl.ds(place, LOOK_AZ), q * dates : (q + 1) * dates
                     ] = value[:, side * dates : (side + 1) * dates].reshape(cells, LOOK_AZ, dates)
         return carry
@@ -194,47 +215,45 @@
 
     lax.fori_loop(0, PHASES, one_phase, 0)
 
-
-def cells_kernel(first_ref, second_ref, pixels_ref, coherence_ref, chosen_ref):
-    dates = pixels_ref.shape[2] // 2
-    eye = lax.broadcasted_iota(jnp.int32, (dates, dates), 0) == lax.broadcasted_iota(
-        jnp.int32, (dates, dates), 1
-    )
-    for g in range(pixels_ref.shape[0]):
-        pixels = pixels_ref[g]
-        gram = lax.dot_general(
-            pixels, pixels, (((0,), (0,)), ((), ())), preferred_element_type=jnp.float32
-        )
-        real = gram[:dates, :dates] + gram[dates:, dates:]
-        imag = gram[dates:, :dates] - gram[:dates, dates:]
-        diagonal = jnp.where(eye, real, 0.0)
-        row = lax.rsqrt(jnp.sum(diagonal, 0, keepdims=True) + damping)
-        column = lax.rsqrt(jnp.sum(diagonal, 1, keepdims=True) + damping)
-        scale = row * column
-        for q, value in enumerate((real, imag)):
-            gamma = (value * scale).astype(jnp.bfloat16)
-            coherence_ref[g, q] = gamma
-            picked = jnp.dot(gamma, second_ref[...], preferred_element_type=jnp.float32)
-            chosen_ref[q, g : g + 1, :] = jnp.sum(picked * first_ref[...], 0, keepdims=True)
-
-
-def ramps_kernel(n, chosen_ref, flat_ref, ramps_ref, sums, sum_send, sum_recv):
-    me = lax.axis_index("wide")
-    cells, pairs = chosen_ref.shape[1], chosen_ref.shape[2]
-    barrier = pltpu.get_barrier_semaphore()
-
-    def other(k):
-        return lax.rem(me + k, n)
-
-    def greet(k, carry):
-        pl.semaphore_signal(barrier, inc=1, device_id={"wide": other(k)}, device_id_type=pl.DeviceIdType.MESH)
-        return carry
-
-    lax.fori_loop(1, n, greet, 0)
+    batch = 8
+    pair_count = pairs_ref.shape[1]
+    date = lax.broadcasted_iota(jnp.int32, (dates, pair_count), 0)
+    first = jnp.where(date == pairs_ref[0:1, :], 1.0, 0.0)
+    second = jnp.where(date == pairs_ref[1:2, :], 1.0, 0.0).astype(jnp.bfloat16)
+
+    def result_copy(b):
+        block = pl.ds(b * batch, batch)
+        return pltpu.make_async_copy(coherent.at[block], coherence_ref.at[block], out_sem.at[b])
+
+    def cell_batch(b, carry):
+        picks = [[], []]
+        for i in range(batch):
+            g = b * batch + i
+            pixels = pixels_ref[g]
+            gram = lax.dot_general(
+                pixels, pixels, (((0,), (0,)), ((), ())), preferred_element_type=jnp.float32
+            )
+            real = gram[:dates, :dates] + gram[dates:, dates:]
+            imag = gram[dates:, :dates] - gram[:dates, dates:]
+            diagonal = jnp.where(eye, real, 0.0)
+            row_scale = lax.rsqrt(jnp.sum(diagonal, 0, keepdims=True) + damping)
+            column_scale = lax.rsqrt(jnp.sum(diagonal, 1, keepdims=True) + damping)
+            scale = row_scale * column_scale
+            for q, value in enumerate((real, imag)):
+                gamma = (value * scale).astype(jnp.bfloat16)
+                coherent[g, q] = gamma
+                picked = jnp.dot(gamma, second, preferred_element_type=jnp.float32)
+                picks[q].append(jnp.sum(picked * first, 0, keepdims=True))
+        for q in range(2):
+            chosen[q, pl.ds(pl.multiple_of(b * batch, batch), batch), :] = jnp.concatenate(picks[q], 0)
+        result_copy(b).start()
+        return carry
+
+    lax.fori_loop(0, LINE_CELLS // batch, cell_batch, 0)
     across = (
-        lax.broadcasted_iota(jnp.int32, (cells, pairs), 0).astype(jnp.float32) + 0.5
-    ) / cells - 0.5
-    real, imag = chosen_ref[0], chosen_ref[1]
+        lax.broadcasted_iota(jnp.int32, (LINE_CELLS, pair_count), 0).astype(jnp.float32) + 0.5
+    ) / LINE_CELLS - 0.5
+    real, imag = chosen[0], chosen[1]
     weights = 0.1 + real * real + imag * imag
     tilted = weights * across
 
@@ -246,12 +265,10 @@
             down(weights), down(tilted), down(tilted * across),
             down(weights * real), down(tilted * real),
             down(weights * imag), down(tilted * imag),
-            jnp.zeros((1, pairs), jnp.float32),
+            jnp.zeros((1, pair_count), jnp.float32),
         ],
         0,
     )
-    pl.semaphore_wait(barrier, n - 1)
-
     def sum_copy(k):
         return pltpu.make_async_remote_copy(
             src_ref=sums.at[me], dst_ref=sums.at[me],
@@ -259,17 +276,17 @@
             device_id={"wide": other(k)}, device_id_type=pl.DeviceIdType.MESH,
         )
 
-    def start(k, carry):
+    def start_sum(k, carry):
         sum_copy(k).start()
         return carry
 
-    def finish(k, carry):
+    def finish_sum(k, carry):
         sum_copy(k).wait()
         return carry
 
-    lax.fori_loop(1, n, start, 0)
-    lax.fori_loop(1, n, finish, 0)
-    plain = jnp.zeros((8, pairs), jnp.float32)
+    lax.fori_loop(1, n, start_sum, 0)
+    lax.fori_loop(1, n, finish_sum, 0)
+    plain = jnp.zeros((8, pair_count), jnp.float32)
     once = plain
     twice = plain
     for source in range(n):
@@ -298,7 +315,23 @@
         b2 = (adj02 * t0 + adj12 * t1 + adj22 * t2) / determinant
         rows += [b0, b1, b2]
         flat_ref[:, q, :] = value - (b0 + across * b1 + my_along * b2)
-    ramps_ref[...] = jnp.concatenate(rows + [jnp.zeros((2, pairs), jnp.float32)], 0)
+    solved = jnp.concatenate(rows + [jnp.zeros((2, pair_count), jnp.float32)], 0)
+    pairs_here = ramps_ref.shape[0]
+    lane = lax.broadcasted_iota(jnp.int32, (8, pair_count), 1)
+    line = lax.broadcasted_iota(jnp.int32, (8, pair_count), 0)
+    chooser = jnp.where(lane == me * pairs_here + line, 1.0, 0.0)
+    own_ramps = lax.dot_general(
+        chooser, solved, (((1,), (1,)), ((), ())),
+        precision=lax.Precision.HIGHEST, preferred_element_type=jnp.float32,
+    )
+    for q in range(2):
+        ramps_ref[:, q, :] = own_ramps[:pairs_here, 3 * q : 3 * q + 3]
+
+    def finish_result(b, carry):
+        result_copy(b).wait()
+        return carry
+
+    lax.fori_loop(0, LINE_CELLS // batch, finish_result, 0)
 
 
 def local(slc, offsets, row_start, row_stop, pairs):
@@ -316,70 +349,45 @@
     forward, inverse = host_tables()
     vmem = pl.BlockSpec(memory_space=pltpu.VMEM)
     anywhere = pl.BlockSpec(memory_space=pl.ANY)
-    pixels = pl.pallas_call(
-        functools.partial(resample_kernel, n),
-        out_shape=jax.ShapeDtypeStruct((LINE_CELLS, columns * LOOK_AZ, 2 * dates), jnp.bfloat16),
-        in_specs=[anywhere, anywhere] + [vmem] * 6,
-        out_specs=vmem,
+    far = pl.BlockSpec(memory_space=pltpu.HBM)
+    coherence, flattened, ramps = pl.pallas_call(
+        functools.partial(stack_kernel, n),
+        out_shape=[
+            jax.ShapeDtypeStruct((LINE_CELLS, 2, dates, dates), jnp.bfloat16),
+            jax.ShapeDtypeStruct((LINE_CELLS, 2, pair_count), jnp.float32),
+            jax.ShapeDtypeStruct((pair_count // n, 2, 3), jnp.float32),
+        ],
+        in_specs=[anywhere] * 2 + [far] * 3 + [vmem] * 3,
+        out_specs=[anywhere, vmem, vmem],
         scratch_shapes=[
             pltpu.VMEM((dates, columns, RADIX, 2, PART), jnp.bfloat16),
             pltpu.VMEM((n, columns, dates), jnp.bfloat16),
             pltpu.VMEM((columns, dates), jnp.float32),
             pltpu.VMEM((dates, AZ), jnp.float32),
+            pltpu.VMEM((LINE_CELLS, columns * LOOK_AZ, 2 * dates), jnp.bfloat16),
+            pltpu.VMEM((LINE_CELLS, 2, dates, dates), jnp.bfloat16),
+            pltpu.VMEM((2, LINE_CELLS, pair_count), jnp.float32),
+            pltpu.VMEM((n, 8, pair_count), jnp.float32),
+            pltpu.VMEM((2 * dates, 2 * dates), jnp.bfloat16),
+            pltpu.VMEM(forward.shape, jnp.bfloat16),
+            pltpu.VMEM(inverse.shape, jnp.bfloat16),
             pltpu.SemaphoreType.DMA((PHASES, n)),
             pltpu.SemaphoreType.DMA((PHASES, n)),
             pltpu.SemaphoreType.DMA((n,)),
             pltpu.SemaphoreType.DMA((n,)),
-            pltpu.SemaphoreType.DMA((2,)),
+            pltpu.SemaphoreType.DMA((5,)),
+            pltpu.SemaphoreType.DMA((LINE_CELLS // 8,)),
+            pltpu.SemaphoreType.DMA((n,)),
+            pltpu.SemaphoreType.DMA((n,)),
         ],
         compiler_params=pltpu.CompilerParams(
             collective_id=0, has_side_effects=True, vmem_limit_bytes=48 << 20
         ),
     )(
         samples, placed, split_table(dates), forward, inverse, frequency_factors(),
-        row_start[:, None], row_stop[:, None],
-    )
-
-    date = jnp.arange(dates, dtype=jnp.int32)[:, None]
-    first = (date == pairs[:, 0][None, :]).astype(jnp.float32)
-    second = (date == pairs[:, 1][None, :]).astype(jnp.bfloat16)
-    batch = 8
-    coherent, chosen = pl.pallas_call(
-        cells_kernel,
-        grid=(LINE_CELLS // batch,),
-        in_specs=[
-            pl.BlockSpec((dates, pair_count), lambda i: (0, 0)),
-            pl.BlockSpec((dates, pair_count), lambda i: (0, 0)),
-            pl.BlockSpec((batch, columns * LOOK_AZ, 2 * dates), lambda i: (i, 0, 0)),
-        ],
-        out_specs=[
-            pl.BlockSpec((batch, 2, dates, dates), lambda i: (i, 0, 0, 0)),
-            pl.BlockSpec((2, batch, pair_count), lambda i: (0, i, 0)),
-        ],
-        out_shape=[
-            jax.ShapeDtypeStruct((LINE_CELLS, 2, dates, dates), jnp.bfloat16),
-            jax.ShapeDtypeStruct((2, LINE_CELLS, pair_count), jnp.float32),
-        ],
-    )(first, second, pixels)
-
-    flattened, ramps = pl.pallas_call(
-        functools.partial(ramps_kernel, n),
-        in_specs=[vmem],
-        out_specs=[vmem, vmem],
-        out_shape=[
-            jax.ShapeDtypeStruct((LINE_CELLS, 2, pair_count), jnp.float32),
-            jax.ShapeDtypeStruct((8, pair_count), jnp.float32),
-        ],
-        scratch_shapes=[
-            pltpu.VMEM((n, 8, pair_count), jnp.float32),
-            pltpu.SemaphoreType.DMA((n,)),
-            pltpu.SemaphoreType.DMA((n,)),
-        ],
-        compiler_params=pltpu.CompilerParams(collective_id=1, has_side_effects=True),
-    )(chosen)
-    pairs_here = pair_count // n
-    own = lax.dynamic_slice_in_dim(ramps, me * pairs_here, pairs_here, 1)[:6]
-    return coherent, flattened, own.T.reshape(pairs_here, 2, 3)
+        jnp.stack([row_start, row_stop]), pairs.T,
+    )
+    return coherence, flattened, ramps
 
 
 def solution(mesh):

time: 132 us -> 124 us (0.939)
  Pallas kernels: 119 us -> 115 us
  local copies, waits for them, and re-layouts: 10.8 us -> 7.11 us
    pallas_call x3 -> x1, Pallas kernels: 119 us -> 115 us  [local(): pl.pallas_call(functools.partial(stack_kernel, n), out_shape=[jax.ShapeDt...]
    broadcast_in_dim x2 -> x0, local copies, waits for them, and re-layouts: 1.53 us -> none  [the longest x1 0.77 us: local(): row_start[:, None]]
where the time goes in v1:
time: 124 us
  Pallas kernels  115 us (93%)
  local copies, waits for them, and re-layouts  7.11 us (6%)
    pallas_call x1, Pallas kernels, local(): pl.pallas_call(functools.partial(stack_kernel, n), out_shape=[jax.ShapeDt...  115 us
    unnamed x14, local copies, waits for them, and re-layouts  6.32 us

profile of v1, /device:TPU:0, one launch (start us, length us, event | category | flops | bytes accessed | tf_op | source)
XLA Modules:
  0.0 123.9 jit_solution(14489599257698736002)
XLA Ops:
  0.6 0.0 copy-start
  0.7 0.7 pad_add_fusion.bounds_ref
  1.3 0.0 copy-done
  1.3 0.3 fusion
  1.6 0.1 copy.12
  1.8 0.0 copy-start.1
  1.8 1.0 copy-done.1
  2.8 0.0 copy-start.2
  2.8 1.0 copy-done.2
  3.8 0.0 copy-start.3
  3.8 0.9 copy-done.3
  4.7 0.0 copy-start.4
  4.8 0.7 copy-done.4
  5.5 0.0 copy-start.5
  5.5 0.7 copy-done.5
  6.1 115.2 %shard_map.112 = (bf16[32,2,128,128]{3,2,1,0:T(8,128)(2,1)S(1)}, f32[32,2,64]{2,1,0:T(2,128)S(1)}, f32[4,2,3]{2,1,0:T(2,128)S(1)}) custom-call(bf16[8,256,4,2,128]{4,3,2,1,0:T(2,128)(2,1)} %bitcast.12, bf16[16,16,128]{2,1,0:T(8,128)(2,1)S(1)} %bitcast.10, bf16[256,256]{1,0:T(8,128)(2,1)S(1)} %copy-done.3, bf16[4,256,256]{2,1,0:T(8,128)(2,1)S(1)} %copy-done.2, ...), custom_call_target="tpu_custom_call" | custom-call | tf_op jit(solution)/shard_map/pallas_call | solution.py:353
  121.3 0.7 copy.13
  122.0 1.3 %copy.16 = bf16[32,2,128,128]{3,2,1,0:T(8,128)(2,1)} copy(bf16[32,2,128,128]{3,2,1,0:T(8,128)(2,1)S(1)} %get-tuple-element.9) | data formatting | bytes 4194304
  123.3 0.6 copy.17
  (1 shorter events, 0.0 us)
Async XLA Ops:
  0.6 0.7 copy-start
  1.8 1.1 copy-start.1
  2.8 1.0 copy-start.2
  3.8 0.9 copy-start.3
  4.7 0.7 copy-start.4
  5.5 0.7 copy-start.5

commit v2 on v1

--- a/solution.py
+++ b/solution.py
@@ -3,7 +3,6 @@
 
 import jax
 import jax.numpy as jnp
-import numpy as np
 from jax import lax
 from jax.experimental import pallas as pl
 from jax.experimental.pallas import tpu as pltpu
@@ -22,39 +21,36 @@
 damping = 1.0
 
 
-def host_tables():
-    forward, inverse = [], []
-    m = np.arange(PART)
+def fill_tables(split_ref, forward_ref, inverse_ref):
+    shape = split_ref.shape
+    dates = shape[0] // 2
+    row = lax.broadcasted_iota(jnp.int32, shape, 0)
+    column = lax.broadcasted_iota(jnp.int32, shape, 1)
+    target = jnp.where(row < dates, 2 * row, 2 * (row - dates) + 1)
+    split_ref[...] = jnp.where(column == target, 1.0, 0.0).astype(jnp.bfloat16)
+    m = lax.broadcasted_iota(jnp.int32, (PART, PART), 0)
+    line = lax.broadcasted_iota(jnp.int32, (PART, PART), 1)
     for r in range(RADIX):
-        product = ((RADIX * m + r)[:, None] * m[None, :]) % AZ
-        angles = product * (2.0 * math.pi / AZ)
-        cosine, sine = np.cos(angles), np.sin(angles)
-        forward.append(np.block([[cosine, sine], [-sine, cosine]]))
-        inverse.append(np.block([[cosine.T, -sine.T], [sine.T, cosine.T]]))
-    forward = jnp.asarray(np.stack(forward), jnp.float32).astype(jnp.bfloat16)
-    inverse = jnp.asarray(np.stack(inverse), jnp.float32).astype(jnp.bfloat16)
-    inverse = inverse * jnp.asarray(1.0 / AZ, jnp.bfloat16)
-    return forward, inverse
-
-
-def split_table(dates):
-    table = np.zeros((2, dates, dates, 2), np.float32)
-    for q in range(2):
-        table[q, np.arange(dates), np.arange(dates), q] = 1.0
-    return jnp.asarray(table.reshape(2 * dates, 2 * dates)).astype(jnp.bfloat16)
+        angle = lax.rem((RADIX * m + r) * line, AZ).astype(jnp.float32) * (2.0 * math.pi / AZ)
+        cosine, sine = jnp.cos(angle), jnp.sin(angle)
+        table = jnp.concatenate(
+            [jnp.concatenate([cosine, sine], 1), jnp.concatenate([-sine, cosine], 1)], 0
+        )
+        forward_ref[r] = table.astype(jnp.bfloat16)
+        inverse_ref[r] = (table.T * (1.0 / AZ)).astype(jnp.bfloat16)
 
 
 def frequency_factors():
-    high = np.arange(HIGH)
-    high = np.where(high < HIGH // 2, high, high - HIGH) * (RADIX * LOW)
-    low = np.arange(LOW) * RADIX
-    rest = np.concatenate([np.arange(RADIX), np.zeros(4)])
-    factors = np.concatenate([high, low, rest]).astype(np.float32)
-    return jnp.asarray(factors[:, None])
+    place = lax.broadcasted_iota(jnp.int32, (HIGH + LOW + 8, 1), 0)
+    high = jnp.where(place < HIGH // 2, place, place - HIGH) * (RADIX * LOW)
+    low = (place - HIGH) * RADIX
+    rest = place - (HIGH + LOW)
+    factors = jnp.where(place < HIGH, high, jnp.where(place < HIGH + LOW, low, rest))
+    return factors.astype(jnp.float32)
 
 
 def stack_kernel(
-    n, slc_ref, placed_ref, split_hbm, forward_hbm, inverse_hbm, factor_ref, bounds_ref, pairs_ref,
+    n, pair_count, slc_ref, placed_ref, small_ref,
     coherence_ref, flat_ref, ramps_ref,
     held, shifts, theta, mask, pixels_ref, coherent, chosen, sums, split_ref, forward_ref, inverse_ref,
     send_sem, recv_sem, osend_sem, orecv_sem, own_sem, out_sem, sum_send, sum_recv,
@@ -77,14 +73,6 @@
         return carry
 
     lax.fori_loop(1, n, greet, 0)
-    tables = [
-        pltpu.make_async_copy(source, target, own_sem.at[2 + i])
-        for i, (source, target) in enumerate(
-            ((split_hbm, split_ref), (forward_hbm, forward_ref), (inverse_hbm, inverse_ref))
-        )
-    ]
-    for table in tables:
-        table.start()
     mine = pl.ds(me * dates_here, dates_here)
     own = pltpu.make_async_copy(
         slc_ref.at[:, pl.ds(me * columns, columns)], held.at[mine], own_sem.at[0]
@@ -121,19 +109,19 @@
         return carry
 
     lax.fori_loop(0, PHASES * (n - 1), start_sample, 0)
+    fill_tables(split_ref, forward_ref, inverse_ref)
     eye = lax.broadcasted_iota(jnp.int32, (dates, dates), 0) == lax.broadcasted_iota(
         jnp.int32, (dates, dates), 1
     )
     bounds = [
-        jnp.sum(jnp.where(eye, bounds_ref[i : i + 1, :].astype(jnp.float32), 0.0), 1, keepdims=True)
+        jnp.sum(jnp.where(eye, small_ref[i : i + 1, :dates].astype(jnp.float32), 0.0), 1, keepdims=True)
         for i in range(2)
     ]
     row = lax.broadcasted_iota(jnp.int32, (dates, AZ), 1).astype(jnp.float32)
     mask[...] = jnp.where((row >= bounds[0]) & (row < bounds[1]), 1.0, 0.0)
     own.wait()
     own_shift.wait()
-    for table in tables:
-        table.wait()
+    factors = frequency_factors()
 
     def wait_shift(k, carry):
         shift_copy(k).wait()
@@ -164,7 +152,7 @@
             [theta[pl.ds(pair * 2, 1), :], theta[pl.ds(pair * 2 + 1, 1), :]], 1
         )
         wide = angle.shape[1]
-        rotation = factor_ref[...] * angle
+        rotation = factors * angle
         cosine, sine = jnp.cos(rotation), jnp.sin(rotation)
         hc, hs = cosine[:HIGH][:, None, :], sine[:HIGH][:, None, :]
         lc, ls = cosine[HIGH : HIGH + LOW][None], sine[HIGH : HIGH + LOW][None]
@@ -216,10 +204,9 @@
     lax.fori_loop(0, PHASES, one_phase, 0)
 
     batch = 8
-    pair_count = pairs_ref.shape[1]
     date = lax.broadcasted_iota(jnp.int32, (dates, pair_count), 0)
-    first = jnp.where(date == pairs_ref[0:1, :], 1.0, 0.0)
-    second = jnp.where(date == pairs_ref[1:2, :], 1.0, 0.0).astype(jnp.bfloat16)
+    first = jnp.where(date == small_ref[2:3, :pair_count], 1.0, 0.0)
+    second = jnp.where(date == small_ref[3:4, :pair_count], 1.0, 0.0).astype(jnp.bfloat16)
 
     def result_copy(b):
         block = pl.ds(b * batch, batch)
@@ -239,11 +226,12 @@
             row_scale = lax.rsqrt(jnp.sum(diagonal, 0, keepdims=True) + damping)
             column_scale = lax.rsqrt(jnp.sum(diagonal, 1, keepdims=True) + damping)
             scale = row_scale * column_scale
-            for q, value in enumerate((real, imag)):
-                gamma = (value * scale).astype(jnp.bfloat16)
-                coherent[g, q] = gamma
-                picked = jnp.dot(gamma, second, preferred_element_type=jnp.float32)
-                picks[q].append(jnp.sum(picked * first, 0, keepdims=True))
+            gamma = jnp.concatenate([real * scale, imag * scale], 0).astype(jnp.bfloat16)
+            picked = jnp.dot(gamma, second, preferred_element_type=jnp.float32)
+            for q in range(2):
+                part = slice(q * dates, (q + 1) * dates)
+                coherent[g, q] = gamma[part]
+                picks[q].append(jnp.sum(picked[part] * first, 0, keepdims=True))
         for q in range(2):
             chosen[q, pl.ds(pl.multiple_of(b * batch, batch), batch), :] = jnp.concatenate(picks[q], 0)
         result_copy(b).start()
@@ -346,18 +334,25 @@
     onehot = (spot == jnp.arange(dates, dtype=jnp.int32)[None, :]).astype(jnp.bfloat16)
     placed = jnp.einsum("dc,dl->cl", offsets, onehot, preferred_element_type=jnp.float32)
     placed = placed.astype(jnp.bfloat16).reshape(n, columns, dates)
-    forward, inverse = host_tables()
+    width = max(dates, pair_count)
+    small = jnp.concatenate(
+        [
+            jnp.pad(row_start[None], ((0, 0), (0, width - dates))),
+            jnp.pad(row_stop[None], ((0, 0), (0, width - dates))),
+            jnp.pad(pairs.T, ((0, 0), (0, width - pair_count))),
+        ],
+        0,
+    )
     vmem = pl.BlockSpec(memory_space=pltpu.VMEM)
     anywhere = pl.BlockSpec(memory_space=pl.ANY)
-    far = pl.BlockSpec(memory_space=pltpu.HBM)
     coherence, flattened, ramps = pl.pallas_call(
-        functools.partial(stack_kernel, n),
+        functools.partial(stack_kernel, n, pair_count),
         out_shape=[
             jax.ShapeDtypeStruct((LINE_CELLS, 2, dates, dates), jnp.bfloat16),
             jax.ShapeDtypeStruct((LINE_CELLS, 2, pair_count), jnp.float32),
             jax.ShapeDtypeStruct((pair_count // n, 2, 3), jnp.float32),
         ],
-        in_specs=[anywhere] * 2 + [far] * 3 + [vmem] * 3,
+        in_specs=[anywhere] * 2 + [vmem],
         out_specs=[anywhere, vmem, vmem],
         scratch_shapes=[
             pltpu.VMEM((dates, columns, RADIX, 2, PART), jnp.bfloat16),
@@ -369,13 +364,13 @@
             pltpu.VMEM((2, LINE_CELLS, pair_count), jnp.float32),
             pltpu.VMEM((n, 8, pair_count), jnp.float32),
             pltpu.VMEM((2 * dates, 2 * dates), jnp.bfloat16),
-            pltpu.VMEM(forward.shape, jnp.bfloat16),
-            pltpu.VMEM(inverse.shape, jnp.bfloat16),
+            pltpu.VMEM((RADIX, 2 * PART, 2 * PART), jnp.bfloat16),
+            pltpu.VMEM((RADIX, 2 * PART, 2 * PART), jnp.bfloat16),
             pltpu.SemaphoreType.DMA((PHASES, n)),
             pltpu.SemaphoreType.DMA((PHASES, n)),
             pltpu.SemaphoreType.DMA((n,)),
             pltpu.SemaphoreType.DMA((n,)),
-            pltpu.SemaphoreType.DMA((5,)),
+            pltpu.SemaphoreType.DMA((2,)),
             pltpu.SemaphoreType.DMA((LINE_CELLS // 8,)),
             pltpu.SemaphoreType.DMA((n,)),
             pltpu.SemaphoreType.DMA((n,)),
@@ -384,8 +379,7 @@
             collective_id=0, has_side_effects=True, vmem_limit_bytes=48 << 20
         ),
     )(
-        samples, placed, split_table(dates), forward, inverse, frequency_factors(),
-        jnp.stack([row_start, row_stop]), pairs.T,
+        samples, placed, small,
     )
     return coherence, flattened, ramps
 

time: 124 us -> 122 us (0.984)
  local copies, waits for them, and re-layouts: 7.11 us -> 2.73 us
  Pallas kernels: 115 us -> 117 us
    unnamed x14 -> x4, local copies, waits for them, and re-layouts: 6.32 us -> 1.94 us
    pallas_call x1, Pallas kernels: 115 us -> 117 us  [local(): pl.pallas_call(functools.partial(stack_kernel, n, pair_count), out_shape=...]
where the time goes in v2:
time: 122 us; the launch traced here: 121 us
  Pallas kernels  117 us (96%)
  local copies, waits for them, and re-layouts  2.73 us (2%)
    pallas_call x1, Pallas kernels, local(): pl.pallas_call(functools.partial(stack_kernel, n, pair_count), out_shape=...  117 us

profile of v2, /device:TPU:0, one launch (start us, length us, event | category | flops | bytes accessed | tf_op | source)
XLA Modules:
  0.0 121.4 jit_solution(4978621100978559284)
XLA Ops:
  0.6 0.0 copy-start
  0.7 0.7 pad_add_fusion.small_ref
  1.4 0.0 copy-done
  1.4 0.3 fusion
  1.7 0.1 copy.8
  1.8 117.0 %shard_map.76 = (bf16[32,2,128,128]{3,2,1,0:T(8,128)(2,1)S(1)}, f32[32,2,64]{2,1,0:T(2,128)S(1)}, f32[4,2,3]{2,1,0:T(2,128)S(1)}) custom-call(bf16[8,256,4,2,128]{4,3,2,1,0:T(2,128)(2,1)} %bitcast.11, bf16[16,16,128]{2,1,0:T(8,128)(2,1)S(1)} %bitcast.10, s32[4,128]{1,0:T(4,128)S(1)} %pad_add_fusion.small_ref), custom_call_target="tpu_custom_call" | custom-call | tf_op jit(solution)/shard_map/pallas_call | solution.py:348
  118.8 0.7 copy.9
  119.5 1.3 %copy.12 = bf16[32,2,128,128]{3,2,1,0:T(8,128)(2,1)} copy(bf16[32,2,128,128]{3,2,1,0:T(8,128)(2,1)S(1)} %get-tuple-element.9) | data formatting | bytes 4194304
  120.8 0.6 copy.13
  (1 shorter events, 0.0 us)
Async XLA Ops:
  0.6 0.7 copy-start
